TPU v7x, 512 devices: a whole 4x8x8 slice. The times are simulated.
512 devices in a mesh: stream: 8 (over y), span: 16 (over z, core), vert: 4 (over x).
Axes of the slice: x: 4, y: 8, z: 8, core: 2. Of those that a mesh axis runs over, the one named last changes fastest.
Arguments:
- fields: float32 [5, 128, 256, 1024], P(None, 'vert', 'span', 'stream'), may hold values from -6 to 6
- solid_frac: float32 [128, 256, 1024], P('vert', 'span', 'stream'), may hold values from 0 to 1
- panels: float32 [32768, 5, 256], P(('stream', 'span', 'vert')), may hold values from -0.015625 to 0.015625
- panel_owner: int32 [32768, 1], P(('stream', 'span', 'vert')), may hold values from 0 to 63; in each aligned block of 64 rows (0 to 63, 64 to 127, ...) at most 2 rows name the same one
- deck_cells: int32 [4, 16, 8, 2048], P('vert', 'span', 'stream'), may hold values from 0 to 65535
- deck_geom: float32 [4, 16, 8, 3, 2048], P('vert', None, 'stream'), may hold values from -6 to 6
- strip_ids: int32 [4, 16, 8, 2048], P('vert', None, 'stream'), may hold values from 0 to 63, as said below
- mode_shapes: float32 [3, 64, 32], replicated, may hold values from -0.0034179688 to 0.0034179688
Outputs:
- new_fields: float32 [5, 128, 256, 1024], P(None, 'vert', 'span', 'stream')
- modal_force: float32 [32], replicated
Inputs may be any that keep to these rules, and one draw needn't show every extreme that they name: `panel_owner`: tile number s * 4 + v for along-deck tile s and vertical tile v. Among the 64 panels of one device no tile is named more than 2 times; some device names some tile exactly 2 times. `strip_ids`: cells of along-deck tile s belong to strips s * 4 to (s + 1) * 4 - 1.
All inputs are finite; a program needn't handle non-finite values.
Results may differ from a plain program's by a relative error of at most 0.00012.
Values sent between devices are 32-bit elements; how exact they have to be, the bound alone decides.
No kernel may reach another device: no remote copies, remote signals or barrier semaphores. Data moves between devices by JAX's collectives and lax.ppermute only.
A program may use at most 128 MiB of HBM per device.

v0:
```python
import math
import jax
import jax.numpy as jnp
from jax import lax
from jax.sharding import PartitionSpec as P

CAP = 2
time_step = 0.15
viscous = 0.05
heat_diff = 0.03
sound_sq = 1.0
buoyant = 0.5
penalty = 0.5
relax_time = 0.5
relax_depth = 8.0
wave_cols = 16


def extended(block, sides, width):
    for axis, dim in sides:
        count = lax.axis_size(axis)
        forward = [(i, i + 1) for i in range(count - 1)]
        backward = [(target, source) for source, target in forward]
        low = lax.ppermute(
            lax.slice_in_dim(block, block.shape[dim] - width, None, axis=dim), axis, forward
        )
        high = lax.ppermute(lax.slice_in_dim(block, 0, width, axis=dim), axis, backward)
        block = jnp.concatenate([low, block, high], axis=dim)
    return block


def wave_basis(heights, widths, total_z, total_y, spec):
    modes = jnp.arange(spec, dtype=jnp.int32)
    across = (modes % wave_cols)[:, None, None]
    upward = (modes // wave_cols)[:, None, None]
    period = total_y * total_z
    phase = (
        across * widths[None, None, :] * total_z + upward * heights[None, :, None] * total_y
    ) % period
    angle = phase.astype(jnp.float32) * (2.0 * math.pi / period)
    return jnp.concatenate([jnp.cos(angle), jnp.sin(angle)], axis=0)


def relax_weights(positions, limit):
    spots = positions.astype(jnp.float32)
    return jnp.where(positions < limit, jnp.exp(-spots / relax_depth) / relax_time, 0.0)


def rates(padded, solid_frac, relax_rate, target_plane):
    centre = padded[:, 1:-1, 1:-1, 1:-1]
    east_side = padded[:, 1:-1, 1:-1, 2:]
    west_side = padded[:, 1:-1, 1:-1, :-2]
    north_side = padded[:, 1:-1, 2:, 1:-1]
    south_side = padded[:, 1:-1, :-2, 1:-1]
    upper_side = padded[:, 2:, 1:-1, 1:-1]
    lower_side = padded[:, :-2, 1:-1, 1:-1]
    grad_x = 0.5 * (east_side - west_side)
    grad_y = 0.5 * (north_side - south_side)
    grad_z = 0.5 * (upper_side - lower_side)
    laplace = (
        east_side + west_side + north_side + south_side + upper_side + lower_side - 6.0 * centre
    )
    speed_x = centre[0]
    speed_y = centre[1]
    speed_z = centre[2]
    carried = speed_x * grad_x + speed_y * grad_y + speed_z * grad_z
    coeffs = jnp.array([viscous, viscous, viscous, viscous, heat_diff], jnp.float32)[
        :, None, None, None
    ]
    damping = solid_frac / penalty
    nudging = relax_rate[None, None, None, :] * (target_plane[:, :, :, None] - centre)
    common = coeffs * laplace - carried + nudging
    extra_terms = jnp.stack(
        [
            -grad_x[3] - damping * speed_x,
            -grad_y[3] - damping * speed_y,
            -grad_z[3] - damping * speed_z + buoyant * centre[4],
            -sound_sq * (grad_x[0] + grad_y[1] + grad_z[2]),
            jnp.zeros_like(speed_x),
        ]
    )
    return common + extra_terms


def pack_slots(flat_panels, target_tile, chosen, tile_count):
    running = jnp.cumsum(chosen, axis=0) - 1
    slot_rank = jnp.sum(chosen * running, axis=1)
    slot_index = target_tile * CAP + slot_rank
    dispatch = (
        slot_index[None, :] == jnp.arange(tile_count * CAP, dtype=jnp.int32)[:, None]
    ).astype(jnp.float32)
    return jnp.dot(dispatch, flat_panels, precision=lax.Precision.HIGHEST)


def strip_forces(traction, labels, strip_count):
    columns = jnp.arange(strip_count, dtype=jnp.int32)

    def add_row(running, item_pair):
        row_values, row_labels = item_pair
        member = (row_labels[:, None] == columns[None, :]).astype(jnp.float32)
        return (running + jnp.dot(row_values, member, precision=lax.Precision.HIGHEST), None)

    start_value = jnp.zeros((traction.shape[1], strip_count), jnp.float32)
    summed, ignored = lax.scan(add_row, start_value, (traction, labels))
    return summed


def on_device(
    fields, solid_frac, panels, panel_owner, deck_cells, deck_geom, strip_ids, mode_shapes
):
    depth_cells = fields.shape[1]
    span_cells = fields.shape[2]
    wind_cells = fields.shape[3]
    n_span = lax.axis_size("span")
    n_vert = lax.axis_size("vert")
    stream_pos = lax.axis_index("stream")
    span_pos = lax.axis_index("span")
    vert_pos = lax.axis_index("vert")
    tile_count = n_span * n_vert
    held_panels = panels.shape[0]
    spec_cols = panels.shape[2]
    flat_panels = panels.reshape(held_panels, 5 * spec_cols)
    target_tile = panel_owner[:, 0]
    chosen = (target_tile[:, None] == jnp.arange(tile_count, dtype=jnp.int32)[None, :]).astype(
        jnp.int32
    )
    outgoing = pack_slots(flat_panels, target_tile, chosen, tile_count)
    arrived = lax.all_to_all(
        outgoing.reshape(tile_count, CAP * 5 * spec_cols),
        ("span", "vert"),
        split_axis=0,
        concat_axis=0,
        tiled=True,
    )
    coeffs = jnp.sum(arrived.reshape(-1, 5 * spec_cols), axis=0)
    coeffs = coeffs.reshape(5, spec_cols)
    heights = vert_pos * depth_cells + jnp.arange(depth_cells, dtype=jnp.int32)
    widths = span_pos * span_cells + jnp.arange(span_cells, dtype=jnp.int32)
    wave_table = wave_basis(
        heights, widths, depth_cells * n_vert, span_cells * n_span, spec_cols // 2
    )
    wave_table = wave_table.reshape(spec_cols, depth_cells * span_cells)
    partial_value = jnp.dot(coeffs, wave_table, precision=lax.Precision.HIGHEST)
    inflow_plane = lax.psum(partial_value, "stream").reshape(5, depth_cells, span_cells)
    target_plane = inflow_plane + jnp.array([1.0, 0.0, 0.0, 0.0, 0.0], jnp.float32)[:, None, None]
    wind_first = stream_pos * wind_cells
    relax_rate = relax_weights(
        wind_first + jnp.arange(wind_cells, dtype=jnp.int32), wind_cells // 2
    )

    def advance(state):
        padded = extended(state, (("stream", 3), ("span", 2), ("vert", 1)), 1)
        return rates(padded, solid_frac, relax_rate, target_plane)

    first_update = fields + time_step * advance(fields)
    second_rate = advance(first_update)
    new_fields = 0.5 * (fields + first_update + time_step * second_rate)
    pressure = new_fields[3].reshape(-1)
    sampled = pressure[deck_cells[0, 0, 0]]
    strip_count = mode_shapes.shape[1]
    rows_all = lax.all_gather(sampled.reshape(1, 1, 1, -1), "span", axis=1, tiled=True)
    traction = rows_all[0, :, 0][:, None, :] * deck_geom[0, :, 0]
    forces = strip_forces(traction, strip_ids[0, :, 0], strip_count)
    modal_part = jnp.einsum("cj,cjm->m", forces, mode_shapes, precision=lax.Precision.HIGHEST)
    modal_force = lax.psum(modal_part, ("stream", "vert"))
    return (new_fields, modal_force)


def solution(mesh):
    return jax.shard_map(
        on_device,
        mesh=mesh,
        in_specs=(
            P(None, "vert", "span", "stream"),
            P("vert", "span", "stream"),
            P(("stream", "span", "vert"), None, None),
            P(("stream", "span", "vert"), None),
            P("vert", "span", "stream", None),
            P("vert", None, "stream", None, None),
            P("vert", None, "stream", None),
            P(),
        ),
        out_specs=(P(None, "vert", "span", "stream"), P()),
        check_vma=False,
    )
```

profile of v0, /device:TPU:64, one launch (start us, length us, event | category | flops | bytes accessed | tf_op | source)
XLA Modules:
  0.0 263.3 jit_solution(5278629360200519969)
XLA Ops:
  0.6 2.2 fusion.52
  3.4 1.3 collective-permute-start
  5.3 4.5 %collective-permute-start.1 = (f32[5,32,16,1]{1,2,3,0:T(8,128)S(1)}, f32[5,32,16,1]{1,2,3,0:T(8,128)S(1)}, u32[]{:S(2)}, u32[]{:S(2)}) collective-permute-start(f32[5,32,16,1]{1,2,3,0:T(8,128)S(1)} %copy.56), channel_id=1, source_target_pairs={{0,64},{64,128},{128,192},{192,256},{256,320},{320,384},{384,448},... | collective-permute-start | bytes 30728 | tf_op jit(solution)/shard_map/ppermute | solution.py:24
  10.7 1.5 all_to_all.8
  12.2 13.3 %all-to-all-start = ((f32[64,1,2560]{2,1,0:T(1,128)}), f32[64,1,2560]{2,1,0:T(1,128)}, u32[]{:S(2)}, u32[]{:S(2)}) async-start(f32[64,1,2560]{2,1,0:T(1,128)} %all_to_all.8), calls=%async_computation | async-start | bytes 1310720 | tf_op jit(solution)/shard_map/all_to_all | solution.py:128
  25.6 0.9 bitcast_multiply_fusion.6
  26.7 1.7 fusion.46
  29.1 1.6 copy.39
  30.7 2.5 pad_maximum_fusion.39
  33.2 2.0 collective-permute-start.2
  35.2 2.3 collective-permute-start.3
  37.5 4.0 %collective-permute-done.2 = f32[5,32,1,130]{3,2,1,0:T(1,128)S(1)} collective-permute-done((f32[5,32,1,130]{3,2,1,0:T(1,128)S(1)}, f32[5,32,1,130]{3,2,1,0:T(1,128)S(1)}, u32[]{:S(2)}, u32[]{:S(2)}) %collective-permute-start.2) | collective-permute-done | bytes 83232 | tf_op jit(solution)/shard_map/ppermute | solution.py:27
  41.5 1.5 collective-permute-done.3
  43.2 1.3 collective-permute-start.4
  44.5 4.7 %collective-permute-start.5 = (f32[5,1,18,130]{3,2,1,0:T(8,128)S(1)}, f32[5,1,18,130]{3,2,1,0:T(8,128)S(1)}, u32[]{:S(2)}, u32[]{:S(2)}) collective-permute-start(f32[5,1,18,130]{3,2,1,0:T(8,128)S(1)} %get-tuple-element.71), channel_id=1, source_target_pairs={{0,1},{1,2},{2,3},{4,5},{5,6},{6,7},{8,9},{9,10},{10,11},{12,13},{... | collective-permute-start | bytes 140408 | tf_op jit(solution)/shard_map/ppermute | solution.py:24
  49.3 1.1 broadcast_multiply_fusion.4
  50.5 1.2 collective-permute-done.5
  51.7 3.2 %broadcast_multiply_fusion.3 = (f32[5,32,16,128]{3,2,1,0:T(8,128)S(1)}, f32[5,32,16,128]{3,2,1,0:T(8,128)S(1)}) fusion(f32[5,1,18,130]{3,2,1,0:T(8,128)S(1)} %collective-permute-done.4, f32[5,32,1,130]{3,2,1,0:T(1,128)S(1)} %collective-permute-done.2, f32[5,32,16,1]{3,2,1,0:T(8,128)S(1)} %copy.37, f32[5,32,16,128]{3,2,1,0:T(8,128)S(1)} %copy-done.1, ...), kind=kLoop, calls=%fused_computation.50 | loop fusion | flops 5242880 | bytes 4212640 | tf_op jit(solution)/shard_map/mul | solution.py:59
  54.9 0.7 fusion.40
  55.7 0.8 fusion.36
  56.4 0.8 fusion.32
  57.2 0.8 fusion.27
  58.7 2.6 %reduce = f32[64,2560]{1,0:T(8,128)S(1)} reduce(f32[64,1,2560]{2,1,0:T(1,128)} %all-to-all-done, f32[]{:T(128)} %constant.123), dimensions={1}, to_apply=%all_to_all.7.reduce_sub_computation | reduce | bytes 1310724 | tf_op jit(solution)/shard_map/all_to_all | solution.py:128
  61.5 1.5 fusion.3
  63.1 30.8 %psum.14 = f32[5,32,16]{2,1,0:T(8,128)S(1)} all-reduce(f32[5,32,16]{2,1,0:T(8,128)S(1)} %reshape.200), channel_id=1, replica_groups=mesh['stream'=8,'span'=16,'vert'=4] {'stream'}, use_global_device_ids=true, to_apply=%region_3.4 | all-reduce | flops 2560 | bytes 20480 | tf_op jit(solution)/shard_map/psum | solution.py:144
  94.0 7.5 %multiply_add_fusion = f32[5,32,16,128]{3,2,1,0:T(8,128)S(1)} fusion(f32[5,32,16,128]{3,2,1,0:T(8,128)S(1)} %copy-done.1, f32[5,32,16,128]{3,2,1,0:T(8,128)} %broadcast_dynamic-update-slice_fusion.1, f32[5,32,16]{2,1,0:T(8,128)S(1)} %broadcast_add_fusion.1, f32[128]{0:T(128)S(1)} %compare_select_fusion.1, f32[32,16,128]{2,1,0:T(8,128)} %get-tuple-element.87, ...), kind=kLoop, calls=%fused_computation.45 | loop fusion | flops 13434880 | bytes 5009844 | tf_op jit(solution)/shard_map/add | solution.py:155
  101.5 1.9 fusion.51
  103.5 1.9 copy.44
  105.4 1.3 collective-permute-start.6
  106.7 1.9 copy.46
  108.5 4.5 %collective-permute-start.7 = (f32[5,32,16,1]{1,2,3,0:T(8,128)S(1)}, f32[5,32,16,1]{1,2,3,0:T(8,128)S(1)}, u32[]{:S(2)}, u32[]{:S(2)}) collective-permute-start(f32[5,32,16,1]{1,2,3,0:T(8,128)S(1)} %copy.46), channel_id=1, source_target_pairs={{0,64},{64,128},{128,192},{192,256},{256,320},{320,384},{384,448},... | collective-permute-start | bytes 30728 | tf_op jit(solution)/shard_map/ppermute | solution.py:24
  113.2 1.6 copy.45
  114.8 1.6 copy.47
  116.4 2.9 %pad_maximum_fusion.36 = (f32[5,32,1,130]{3,2,1,0:T(1,128)S(1)}, f32[5,32,1,130]{3,2,1,0:T(1,128)S(1)}) fusion(f32[5,32,16,1]{3,2,1,0:T(8,128)} %copy.45, f32[5,32,16,128]{3,2,1,0:T(8,128)S(1)} %multiply_add_fusion, f32[5,32,16,1]{3,2,1,0:T(8,128)} %copy.47), kind=kLoop, calls=%fused_computation.118 | loop fusion | flops 83200 | bytes 1497600 | tf_op jit(solution)/shard_map/concatenate | solution.py:28
  119.3 2.1 collective-permute-start.8
  121.4 2.6 collective-permute-start.9
  124.2 3.8 %collective-permute-done.9 = f32[5,32,1,130]{3,2,1,0:T(1,128)S(1)} collective-permute-done((f32[5,32,1,130]{3,2,1,0:T(1,128)S(1)}, f32[5,32,1,130]{3,2,1,0:T(1,128)S(1)}, u32[]{:S(2)}, u32[]{:S(2)}) %collective-permute-start.9) | collective-permute-done | bytes 83232 | tf_op jit(solution)/shard_map/ppermute | solution.py:24
  128.2 1.3 collective-permute-start.10
  129.5 5.0 %collective-permute-start.11 = (f32[5,1,18,130]{3,2,1,0:T(8,128)S(1)}, f32[5,1,18,130]{3,2,1,0:T(8,128)S(1)}, u32[]{:S(2)}, u32[]{:S(2)}) collective-permute-start(f32[5,1,18,130]{3,2,1,0:T(8,128)S(1)} %get-tuple-element.69), channel_id=1, source_target_pairs={{0,1},{1,2},{2,3},{4,5},{5,6},{6,7},{8,9},{9,10},{10,11},{12,13},{... | collective-permute-start | bytes 140408 | tf_op jit(solution)/shard_map/ppermute | solution.py:24
  134.5 1.1 broadcast_multiply_fusion.1
  135.6 1.3 collective-permute-done.11
  136.9 3.1 %broadcast_multiply_fusion = (f32[5,32,16,128]{3,2,1,0:T(8,128)S(1)}, f32[5,32,16,128]{3,2,1,0:T(8,128)S(1)}) fusion(f32[5,1,18,130]{3,2,1,0:T(8,128)S(1)} %collective-permute-done.10, f32[5,32,1,130]{3,2,1,0:T(1,128)S(1)} %collective-permute-done.8, f32[5,32,16,1]{3,2,1,0:T(8,128)S(1)} %copy-done.4, f32[5,32,16,128]{3,2,1,0:T(8,128)S(1)} %multiply_add_fusion, ...), kind=kLoop, calls=%fused_computation.47 | loop fusion | flops 5242880 | bytes 4212640 | tf_op jit(solution)/shard_map/mul | solution.py:59
  140.4 5.0 %add_multiply_fusion = f32[5,32,16,128]{3,2,1,0:T(8,128)S(1)} fusion(f32[5,32,16,128]{3,2,1,0:T(8,128)S(1)} %broadcast_dynamic-update-slice_fusion, f32[5,32,16,128]{3,2,1,0:T(8,128)S(1)} %multiply_add_fusion, f32[5,32,16,128]{3,2,1,0:T(8,128)S(1)} %copy-done.1, f32[32,16,128]{2,1,0:T(8,128)S(1)} %get-tuple-element.82, ...), kind=kLoop, calls=%fused_computation.44 | loop fusion | flops 14090240 | bytes 6320564 | tf_op jit(solution)/shard_map/mul | solution.py:157
  145.4 1.0 copy-done.7
  146.5 11.8 %gather_fusion = f32[2048]{0:T(1024)S(1)} fusion(f32[65536]{0:T(1024)S(1)} %bitcast.150, s32[2048]{0:T(1024)S(1)} %broadcast_clamp_fusion), kind=kCustom, calls=%fused_computation | custom fusion | bytes 24576 | tf_op jit(solution)/shard_map/gather | solution.py:159
  158.2 16.8 %all-gather = f32[32768]{0:T(1024)S(1)} all-gather(f32[2048]{0:T(1024)S(1)} %gather_fusion), channel_id=2, replica_groups=mesh['stream'=8,'span'=16,'vert'=4] {'span'}, dimensions={0}, use_global_device_ids=true | all-gather | bytes 139264 | tf_op jit(solution)/shard_map/all_gather | solution.py:161
  175.2 10.6 %while.11 = (s32[]{:T(128)}, f32[3,64]{1,0:T(4,128)S(1)}, f32[16,3,2048]{2,0,1:T(8,128)S(1)}, s32[16,2048]{1,0:T(8,128)S(1)}, s32[]{:T(128)}, /*index=5*/s32[]{:T(128)}) while((s32[]{:T(128)}, f32[3,64]{1,0:T(4,128)S(1)}, f32[16,3,2048]{2,0,1:T(8,128)S(1)}, s32[16,2048]{1,0:T(8,128)S(1)}, s32[]{:T(128)}, /*index=5*/s32[]{:T(128)}) %tuple.46), condition=%wide.region_5.6_spmd.clone, body=%wide.region_4.5_spmd.clone.sunk | while | flops 4850051 | bytes 99927 | solution.py:104
  186.0 77.3 %psum.15 = f32[32]{0:T(128)} all-reduce(f32[32]{0:T(128)S(1)} %convolution_bitcast_fusion), channel_id=1, replica_groups=mesh['stream'=8,'span'=16,'vert'=4] {'stream','vert'}, use_global_device_ids=true, to_apply=%region_6.7 | all-reduce | flops 32 | bytes 256 | tf_op jit(solution)/shard_map/psum | solution.py:165
  (128 shorter events, 15.2 us)
Async XLA Ops:
  0.6 185.2 %copy-start = (f32[3,64,32]{1,2,0:T(8,128)S(1)}, f32[3,64,32]{1,2,0:T(8,128)}, u32[]{:S(2)}) copy-start(f32[3,64,32]{1,2,0:T(8,128)} %param.20) | copy-start | bytes 73732
  2.8 7.1 %copy-start.14 = (s32[64,1]{0,1:T(1,128)S(1)}, s32[64,1]{0,1:T(1,128)}, u32[]{:S(2)}) copy-start(s32[64,1]{0,1:T(1,128)} %param.16) | copy-start | bytes 772
  2.8 7.4 %copy-start.11 = (f32[64,5,256]{2,0,1:T(8,128)S(1)}, f32[64,5,256]{2,0,1:T(8,128)}, u32[]{:S(2)}) copy-start(f32[64,5,256]{2,0,1:T(8,128)} %param.15) | copy-start | bytes 983044
  3.4 25.0 %collective-permute-start = (f32[5,32,16,1]{1,2,3,0:T(8,128)S(1)}, f32[5,32,16,1]{1,2,3,0:T(8,128)S(1)}, u32[]{:S(2)}, u32[]{:S(2)}) collective-permute-start(f32[5,32,16,1]{1,2,3,0:T(8,128)S(1)} %copy.55), channel_id=1, source_target_pairs={{64,0},{128,64},{192,128},{256,192},{320,256},{384,320},{448,384},... | collective-permute-start | bytes 30728 | tf_op jit(solution)/shard_map/ppermute | solution.py:27
  5.3 23.7 %collective-permute-start.1 = (f32[5,32,16,1]{1,2,3,0:T(8,128)S(1)}, f32[5,32,16,1]{1,2,3,0:T(8,128)S(1)}, u32[]{:S(2)}, u32[]{:S(2)}) collective-permute-start(f32[5,32,16,1]{1,2,3,0:T(8,128)S(1)} %copy.56), channel_id=1, source_target_pairs={{0,64},{64,128},{128,192},{192,256},{256,320},{320,384},{384,448},... | collective-permute-start | bytes 30728 | tf_op jit(solution)/shard_map/ppermute | solution.py:24
  10.7 14.8 %copy-start.1 = (f32[5,32,16,128]{3,2,1,0:T(8,128)S(1)}, f32[5,32,16,128]{3,2,1,0:T(8,128)}, u32[]{:S(2)}) copy-start(f32[5,32,16,128]{3,2,1,0:T(8,128)} %param.13) | copy-start | bytes 3932164
  12.2 14.2 %copy-start.13 = (s32[1,1,1,2048]{3,2,1,0:T(1,128)S(1)}, s32[1,1,1,2048]{3,2,1,0:T(1,128)}, u32[]{:S(2)}) copy-start(s32[1,1,1,2048]{3,2,1,0:T(1,128)} %param.17) | copy-start | bytes 24580
  12.2 46.5 %all-to-all-start = ((f32[64,1,2560]{2,1,0:T(1,128)}), f32[64,1,2560]{2,1,0:T(1,128)}, u32[]{:S(2)}, u32[]{:S(2)}) async-start(f32[64,1,2560]{2,1,0:T(1,128)} %all_to_all.8), calls=%async_computation | async-start | bytes 1310720 | tf_op jit(solution)/shard_map/all_to_all | solution.py:128
  29.1 22.7 %copy-start.2 = (f32[5,32,16,1]{3,2,1,0:T(8,128)}, f32[5,32,16,1]{3,2,1,0:T(8,128)S(1)}, u32[]{:S(2)}) copy-start(f32[5,32,16,1]{3,2,1,0:T(8,128)S(1)} %copy.37) | copy-start | bytes 30724
  30.7 12.4 %copy-start.3 = (f32[5,32,16,1]{3,2,1,0:T(8,128)S(1)}, f32[5,32,16,1]{3,2,1,0:T(8,128)}, u32[]{:S(2)}) copy-start(f32[5,32,16,1]{3,2,1,0:T(8,128)} %copy.39) | copy-start | bytes 30724
  33.2 8.4 %collective-permute-start.2 = (f32[5,32,1,130]{3,2,1,0:T(1,128)S(1)}, f32[5,32,1,130]{3,2,1,0:T(1,128)S(1)}, u32[]{:S(2)}, u32[]{:S(2)}) collective-permute-start(f32[5,32,1,130]{3,2,1,0:T(1,128)S(1)} %get-tuple-element.80), channel_id=1, source_target_pairs={{4,0},{8,4},{12,8},{16,12},{20,16},{24,20},{28,24},{32,28},{36,32}... | collective-permute-start | bytes 249608 | tf_op jit(solution)/shard_map/ppermute | solution.py:27
  35.2 7.9 %collective-permute-start.3 = (f32[5,32,1,130]{3,2,1,0:T(1,128)S(1)}, f32[5,32,1,130]{3,2,1,0:T(1,128)S(1)}, u32[]{:S(2)}, u32[]{:S(2)}) collective-permute-start(f32[5,32,1,130]{3,2,1,0:T(1,128)S(1)} %get-tuple-element.79), channel_id=1, source_target_pairs={{0,4},{4,8},{8,12},{12,16},{16,20},{20,24},{24,28},{28,32},{32,36}... | collective-permute-start | bytes 249608 | tf_op jit(solution)/shard_map/ppermute | solution.py:24
  43.2 7.3 %collective-permute-start.4 = (f32[5,1,18,130]{3,2,1,0:T(8,128)S(1)}, f32[5,1,18,130]{3,2,1,0:T(8,128)S(1)}, u32[]{:S(2)}, u32[]{:S(2)}) collective-permute-start(f32[5,1,18,130]{3,2,1,0:T(8,128)S(1)} %get-tuple-element.72), channel_id=1, source_target_pairs={{1,0},{2,1},{3,2},{5,4},{6,5},{7,6},{9,8},{10,9},{11,10},{13,12},{... | collective-permute-start | bytes 140408 | tf_op jit(solution)/shard_map/ppermute | solution.py:27
  44.5 7.2 %collective-permute-start.5 = (f32[5,1,18,130]{3,2,1,0:T(8,128)S(1)}, f32[5,1,18,130]{3,2,1,0:T(8,128)S(1)}, u32[]{:S(2)}, u32[]{:S(2)}) collective-permute-start(f32[5,1,18,130]{3,2,1,0:T(8,128)S(1)} %get-tuple-element.71), channel_id=1, source_target_pairs={{0,1},{1,2},{2,3},{4,5},{5,6},{6,7},{8,9},{9,10},{10,11},{12,13},{... | collective-permute-start | bytes 140408 | tf_op jit(solution)/shard_map/ppermute | solution.py:24
  50.4 4.5 %copy-start.6 = (f32[32,16,128]{2,1,0:T(8,128)S(1)}, f32[32,16,128]{2,1,0:T(8,128)}, u32[]{:S(2)}) copy-start(f32[32,16,128]{2,1,0:T(8,128)} %param.14) | copy-start | bytes 786436
  50.5 4.4 %copy-start.8 = (f32[5,1,18,130]{3,2,1,0:T(8,128)}, f32[5,1,18,130]{3,2,1,0:T(8,128)S(1)}, u32[]{:S(2)}) copy-start(f32[5,1,18,130]{3,2,1,0:T(8,128)S(1)} %collective-permute-done.4) | copy-start | bytes 140404
  51.7 3.2 %copy-start.9 = (f32[5,1,18,130]{3,2,1,0:T(8,128)}, f32[5,1,18,130]{3,2,1,0:T(8,128)S(1)}, u32[]{:S(2)}) copy-start(f32[5,1,18,130]{3,2,1,0:T(8,128)S(1)} %collective-permute-done.5) | copy-start | bytes 140404
  61.3 32.6 %copy-start.16 = (f32[5]{0:T(128)S(1)}, f32[5]{0:T(128)}, u32[]{:S(2)}) copy-start(f32[5]{0:T(128)} %constant.116.clone) | copy-start | bytes 64
  61.4 32.6 %copy-start.15 = (f32[5]{0:T(128)S(1)}, f32[5]{0:T(128)}, u32[]{:S(2)}) copy-start(f32[5]{0:T(128)} %constant.117.clone) | copy-start | bytes 64
  103.5 9.7 %copy-start.12 = (s32[1,16,1,2048]{3,2,1,0:T(1,128)S(1)}, s32[1,16,1,2048]{3,2,1,0:T(1,128)}, u32[]{:S(2)}) copy-start(s32[1,16,1,2048]{3,2,1,0:T(1,128)} %param.19) | copy-start | bytes 393220
  105.4 7.8 %collective-permute-start.6 = (f32[5,32,16,1]{1,2,3,0:T(8,128)S(1)}, f32[5,32,16,1]{1,2,3,0:T(8,128)S(1)}, u32[]{:S(2)}, u32[]{:S(2)}) collective-permute-start(f32[5,32,16,1]{1,2,3,0:T(8,128)S(1)} %copy.44), channel_id=1, source_target_pairs={{64,0},{128,64},{192,128},{256,192},{320,256},{384,320},{448,384},... | collective-permute-start | bytes 30728 | tf_op jit(solution)/shard_map/ppermute | solution.py:27
  108.5 6.3 %collective-permute-start.7 = (f32[5,32,16,1]{1,2,3,0:T(8,128)S(1)}, f32[5,32,16,1]{1,2,3,0:T(8,128)S(1)}, u32[]{:S(2)}, u32[]{:S(2)}) collective-permute-start(f32[5,32,16,1]{1,2,3,0:T(8,128)S(1)} %copy.46), channel_id=1, source_target_pairs={{0,64},{64,128},{128,192},{192,256},{256,320},{320,384},{384,448},... | collective-permute-start | bytes 30728 | tf_op jit(solution)/shard_map/ppermute | solution.py:24
  116.4 11.6 %copy-start.5 = (f32[5,32,16,1]{3,2,1,0:T(8,128)S(1)}, f32[5,32,16,1]{3,2,1,0:T(8,128)}, u32[]{:S(2)}) copy-start(f32[5,32,16,1]{3,2,1,0:T(8,128)} %copy.47) | copy-start | bytes 30724
  119.3 8.7 %copy-start.4 = (f32[5,32,16,1]{3,2,1,0:T(8,128)S(1)}, f32[5,32,16,1]{3,2,1,0:T(8,128)}, u32[]{:S(2)}) copy-start(f32[5,32,16,1]{3,2,1,0:T(8,128)} %copy.45) | copy-start | bytes 30724
  119.3 4.9 %collective-permute-start.8 = (f32[5,32,1,130]{3,2,1,0:T(1,128)S(1)}, f32[5,32,1,130]{3,2,1,0:T(1,128)S(1)}, u32[]{:S(2)}, u32[]{:S(2)}) collective-permute-start(f32[5,32,1,130]{3,2,1,0:T(1,128)S(1)} %get-tuple-element.76), channel_id=1, source_target_pairs={{4,0},{8,4},{12,8},{16,12},{20,16},{24,20},{28,24},{32,28},{36,32}... | collective-permute-start | bytes 249608 | tf_op jit(solution)/shard_map/ppermute | solution.py:27
  121.4 6.6 %collective-permute-start.9 = (f32[5,32,1,130]{3,2,1,0:T(1,128)S(1)}, f32[5,32,1,130]{3,2,1,0:T(1,128)S(1)}, u32[]{:S(2)}, u32[]{:S(2)}) collective-permute-start(f32[5,32,1,130]{3,2,1,0:T(1,128)S(1)} %get-tuple-element.75), channel_id=1, source_target_pairs={{0,4},{4,8},{8,12},{12,16},{16,20},{20,24},{24,28},{28,32},{32,36}... | collective-permute-start | bytes 249608 | tf_op jit(solution)/shard_map/ppermute | solution.py:24
  128.2 7.4 %collective-permute-start.10 = (f32[5,1,18,130]{3,2,1,0:T(8,128)S(1)}, f32[5,1,18,130]{3,2,1,0:T(8,128)S(1)}, u32[]{:S(2)}, u32[]{:S(2)}) collective-permute-start(f32[5,1,18,130]{3,2,1,0:T(8,128)S(1)} %get-tuple-element.70), channel_id=1, source_target_pairs={{1,0},{2,1},{3,2},{5,4},{6,5},{7,6},{9,8},{10,9},{11,10},{13,12},{... | collective-permute-start | bytes 140408 | tf_op jit(solution)/shard_map/ppermute | solution.py:27
  129.5 7.4 %collective-permute-start.11 = (f32[5,1,18,130]{3,2,1,0:T(8,128)S(1)}, f32[5,1,18,130]{3,2,1,0:T(8,128)S(1)}, u32[]{:S(2)}, u32[]{:S(2)}) collective-permute-start(f32[5,1,18,130]{3,2,1,0:T(8,128)S(1)} %get-tuple-element.69), channel_id=1, source_target_pairs={{0,1},{1,2},{2,3},{4,5},{5,6},{6,7},{8,9},{9,10},{10,11},{12,13},{... | collective-permute-start | bytes 140408 | tf_op jit(solution)/shard_map/ppermute | solution.py:24
  145.4 1.1 copy-start.7
  146.4 28.6 %copy-start.10 = (f32[1,16,1,3,2048]{4,2,3,1,0:T(1,128)S(1)}, f32[1,16,1,3,2048]{4,2,3,1,0:T(1,128)}, u32[]{:S(2)}) copy-start(f32[1,16,1,3,2048]{4,2,3,1,0:T(1,128)} %param.18) | copy-start | bytes 1179652
where the time goes:
time: 264 us; the launch traced here: 263 us
  blocking collectives  125 us (47%)
  starting transfers between devices  46.3 us (18%)
  other arithmetic  36.1 us (14%)
  local copies, waits for them, and re-layouts  30.7 us (12%)
  waiting for transfers between devices  12.1 us (5%)
  matrix products  11.3 us (4%)
    psum x1, blocking collectives, on_device(): modal_force = lax.psum(modal_part, ('stream', 'vert'))  77.3 us
    psum x1, blocking collectives, on_device(): lax.psum(partial_value, 'stream').reshape(5, depth_cells, span_cells)  30.8 us
    ppermute x6, starting transfers between devices, extended(): lax.ppermute(lax.slice_in_dim(block, block.shape[dim] - width, None, axis...  23.8 us
    all_gather x1, blocking collectives, on_device(): lax.all_gather(sampled.reshape(1, 1, 1, -1), 'span', axis=1, tiled=True)  16.8 us
    all_to_all x1, starting transfers between devices, on_device(): lax.all_to_all(outgoing.reshape(tile_count, CAP * 5 * spec_cols), ('span'...  13.3 us
    gather x1, local copies, waits for them, and re-layouts, on_device(): sampled = pressure[deck_cells[0, 0, 0]]  11.8 us
    dot_general x16, matrix products, add_row(): jnp.dot(row_values, member, precision=lax.Precision.HIGHEST)  9.31 us
    ppermute x6, starting transfers between devices, extended(): lax.ppermute(lax.slice_in_dim(block, 0, width, axis=dim), axis, backward)  9.23 us
  transfers between devices with their start and end apart: 13, of which 7 were waited for; matrix products, arithmetic and copies ran while one was open for 8% of the time, Pallas kernels for 0%

commit v1 on v0

--- a/solution.py
+++ b/solution.py
@@ -14,6 +14,11 @@
 relax_time = 0.5
 relax_depth = 8.0
 wave_cols = 16
+
+
+def summed_here(x, axis):
+    parts = lax.all_gather(x, axis)
+    return jnp.sum(parts, axis=0)
 
 
 def extended(block, sides, width):
@@ -141,7 +146,7 @@
     )
     wave_table = wave_table.reshape(spec_cols, depth_cells * span_cells)
     partial_value = jnp.dot(coeffs, wave_table, precision=lax.Precision.HIGHEST)
-    inflow_plane = lax.psum(partial_value, "stream").reshape(5, depth_cells, span_cells)
+    inflow_plane = summed_here(partial_value, "stream").reshape(5, depth_cells, span_cells)
     target_plane = inflow_plane + jnp.array([1.0, 0.0, 0.0, 0.0, 0.0], jnp.float32)[:, None, None]
     wind_first = stream_pos * wind_cells
     relax_rate = relax_weights(

time: 264 us -> 260 us (0.985)
  the two profiles are of different devices: /device:TPU:64 before, /device:TPU:32 now
where the time goes in v1:
time: 260 us; the launch traced here: 259 us
  blocking collectives  124 us (48%)
  starting transfers between devices  47.1 us (18%)
  other arithmetic  36.1 us (14%)
  local copies, waits for them, and re-layouts  30.7 us (12%)
  matrix products  11.3 us (4%)
  waiting for transfers between devices  7.42 us (3%)
    psum x1, blocking collectives, on_device(): modal_force = lax.psum(modal_part, ('stream', 'vert'))  73.9 us
    all_gather x1, blocking collectives, on_device(): lax.all_gather(sampled.reshape(1, 1, 1, -1), 'span', axis=1, tiled=True)  25.7 us
    all_gather x1, blocking collectives, summed_here(): parts = lax.all_gather(x, axis)  24.6 us
    ppermute x6, starting transfers between devices, extended(): lax.ppermute(lax.slice_in_dim(block, block.shape[dim] - width, None, axis...  21.5 us
    all_to_all x1, starting transfers between devices, on_device(): lax.all_to_all(outgoing.reshape(tile_count, CAP * 5 * spec_cols), ('span'...  14.1 us
    gather x1, local copies, waits for them, and re-layouts, on_device(): sampled = pressure[deck_cells[0, 0, 0]]  11.8 us
    ppermute x6, starting transfers between devices, extended(): lax.ppermute(lax.slice_in_dim(block, 0, width, axis=dim), axis, backward)  11.4 us
    dot_general x16, matrix products, add_row(): jnp.dot(row_values, member, precision=lax.Precision.HIGHEST)  9.31 us
  transfers between devices with their start and end apart: 13, of which 5 were waited for; matrix products, arithmetic and copies ran while one was open for 8% of the time, Pallas kernels for 0%

profile of v1, /device:TPU:32, one launch (start us, length us, event | category | flops | bytes accessed | tf_op | source)
XLA Modules:
  0.0 258.8 jit_solution(14789413413344441210)
XLA Ops:
  0.6 2.2 fusion.51
  3.4 2.4 collective-permute-start
  6.4 3.5 %collective-permute-start.1 = (f32[5,32,16,1]{1,2,3,0:T(8,128)S(1)}, f32[5,32,16,1]{1,2,3,0:T(8,128)S(1)}, u32[]{:S(2)}, u32[]{:S(2)}) collective-permute-start(f32[5,32,16,1]{1,2,3,0:T(8,128)S(1)} %copy.56), channel_id=1, source_target_pairs={{0,64},{64,128},{128,192},{192,256},{256,320},{320,384},{384,448},... | collective-permute-start | bytes 30728 | tf_op jit(solution)/shard_map/ppermute | solution.py:29
  10.7 1.5 all_to_all.8
  12.2 14.1 %all-to-all-start = ((f32[64,1,2560]{2,1,0:T(1,128)}), f32[64,1,2560]{2,1,0:T(1,128)}, u32[]{:S(2)}, u32[]{:S(2)}) async-start(f32[64,1,2560]{2,1,0:T(1,128)} %all_to_all.8), calls=%async_computation | async-start | bytes 1310720 | tf_op jit(solution)/shard_map/all_to_all | solution.py:133
  26.4 0.9 bitcast_multiply_fusion.6
  27.5 1.7 fusion.45
  29.9 1.6 copy.39
  31.6 2.5 pad_maximum_fusion.39
  34.0 1.3 collective-permute-start.2
  35.3 3.0 %collective-permute-start.3 = (f32[5,32,1,130]{3,2,1,0:T(1,128)S(1)}, f32[5,32,1,130]{3,2,1,0:T(1,128)S(1)}, u32[]{:S(2)}, u32[]{:S(2)}) collective-permute-start(f32[5,32,1,130]{3,2,1,0:T(1,128)S(1)} %get-tuple-element.79), channel_id=1, source_target_pairs={{0,4},{4,8},{8,12},{12,16},{16,20},{20,24},{24,28},{28,32},{32,36}... | collective-permute-start | bytes 249608 | tf_op jit(solution)/shard_map/ppermute | solution.py:29
  38.4 1.0 collective-permute-done.3
  39.5 1.3 collective-permute-start.4
  40.9 4.7 %collective-permute-start.5 = (f32[5,1,18,130]{3,2,1,0:T(8,128)S(1)}, f32[5,1,18,130]{3,2,1,0:T(8,128)S(1)}, u32[]{:S(2)}, u32[]{:S(2)}) collective-permute-start(f32[5,1,18,130]{3,2,1,0:T(8,128)S(1)} %get-tuple-element.71), channel_id=1, source_target_pairs={{0,1},{1,2},{2,3},{4,5},{5,6},{6,7},{8,9},{9,10},{10,11},{12,13},{... | collective-permute-start | bytes 140408 | tf_op jit(solution)/shard_map/ppermute | solution.py:29
  45.6 1.1 broadcast_multiply_fusion.4
  46.7 1.1 collective-permute-done.5
  47.8 3.2 %broadcast_multiply_fusion.3 = (f32[5,32,16,128]{3,2,1,0:T(8,128)S(1)}, f32[5,32,16,128]{3,2,1,0:T(8,128)S(1)}) fusion(f32[5,1,18,130]{3,2,1,0:T(8,128)S(1)} %collective-permute-done.4, f32[5,32,1,130]{3,2,1,0:T(1,128)S(1)} %collective-permute-done.2, f32[5,32,16,1]{3,2,1,0:T(8,128)S(1)} %copy.37, f32[5,32,16,128]{3,2,1,0:T(8,128)S(1)} %copy-done.1, ...), kind=kLoop, calls=%fused_computation.51 | loop fusion | flops 5242880 | bytes 4212640 | tf_op jit(solution)/shard_map/mul | solution.py:64
  51.0 0.7 fusion.39
  51.8 0.8 fusion.35
  52.5 0.8 fusion.31
  53.3 0.8 fusion.26
  54.8 2.6 %reduce.1 = f32[64,2560]{1,0:T(8,128)S(1)} reduce(f32[64,1,2560]{2,1,0:T(1,128)} %all-to-all-done, f32[]{:T(128)} %constant.123), dimensions={1}, to_apply=%all_to_all.7.reduce_sub_computation | reduce | bytes 1310724 | tf_op jit(solution)/shard_map/all_to_all | solution.py:133
  57.6 1.5 convolution_bitcast_fusion
  59.1 24.6 %all-gather.2 = f32[8,5,512]{2,1,0:T(8,128)S(1)} all-gather(f32[1,5,512]{2,1,0:T(8,128)S(1)} %convolution_bitcast_fusion), channel_id=2, replica_groups=mesh['stream'=8,'span'=16,'vert'=4] {'stream'}, dimensions={0}, use_global_device_ids=true | all-gather | bytes 92160 | tf_op jit(solution)/shard_map/all_gather | solution.py:20
  84.0 7.5 %multiply_add_fusion = f32[5,32,16,128]{3,2,1,0:T(8,128)S(1)} fusion(f32[5,32,16,128]{3,2,1,0:T(8,128)S(1)} %copy-done.1, f32[5,32,16,128]{3,2,1,0:T(8,128)} %broadcast_dynamic-update-slice_fusion.1, f32[5,32,16]{2,1,0:T(8,128)S(1)} %broadcast_add_fusion.1, f32[128]{0:T(128)S(1)} %compare_select_fusion.1, f32[32,16,128]{2,1,0:T(8,128)} %get-tuple-element.87, ...), kind=kLoop, calls=%fused_computation.45 | loop fusion | flops 13434880 | bytes 5009844 | tf_op jit(solution)/shard_map/add | solution.py:160
  91.5 1.9 fusion.50
  93.4 1.9 copy.44
  95.3 3.5 %collective-permute-start.6 = (f32[5,32,16,1]{1,2,3,0:T(8,128)S(1)}, f32[5,32,16,1]{1,2,3,0:T(8,128)S(1)}, u32[]{:S(2)}, u32[]{:S(2)}) collective-permute-start(f32[5,32,16,1]{1,2,3,0:T(8,128)S(1)} %copy.44), channel_id=1, source_target_pairs={{64,0},{128,64},{192,128},{256,192},{320,256},{384,320},{448,384},... | collective-permute-start | bytes 30728 | tf_op jit(solution)/shard_map/ppermute | solution.py:32
  98.9 1.9 copy.46
  100.8 2.3 collective-permute-start.7
  103.1 1.6 copy.45
  104.8 3.1 %collective-permute-done.7 = f32[5,32,16,1]{1,2,3,0:T(8,128)S(1)} collective-permute-done((f32[5,32,16,1]{1,2,3,0:T(8,128)S(1)}, f32[5,32,16,1]{1,2,3,0:T(8,128)S(1)}, u32[]{:S(2)}, u32[]{:S(2)}) %collective-permute-start.7) | collective-permute-done | bytes 10272 | tf_op jit(solution)/shard_map/ppermute | solution.py:29
  107.9 1.6 copy.47
  109.5 2.9 %pad_maximum_fusion.36 = (f32[5,32,1,130]{3,2,1,0:T(1,128)S(1)}, f32[5,32,1,130]{3,2,1,0:T(1,128)S(1)}) fusion(f32[5,32,16,1]{3,2,1,0:T(8,128)} %copy.45, f32[5,32,16,128]{3,2,1,0:T(8,128)S(1)} %multiply_add_fusion, f32[5,32,16,1]{3,2,1,0:T(8,128)} %copy.47), kind=kLoop, calls=%fused_computation.118 | loop fusion | flops 83200 | bytes 1497600 | tf_op jit(solution)/shard_map/concatenate | solution.py:33
  112.4 1.4 collective-permute-start.8
  113.8 3.0 %collective-permute-start.9 = (f32[5,32,1,130]{3,2,1,0:T(1,128)S(1)}, f32[5,32,1,130]{3,2,1,0:T(1,128)S(1)}, u32[]{:S(2)}, u32[]{:S(2)}) collective-permute-start(f32[5,32,1,130]{3,2,1,0:T(1,128)S(1)} %get-tuple-element.75), channel_id=1, source_target_pairs={{0,4},{4,8},{8,12},{12,16},{16,20},{20,24},{24,28},{28,32},{32,36}... | collective-permute-start | bytes 249608 | tf_op jit(solution)/shard_map/ppermute | solution.py:29
  116.9 0.9 collective-permute-done.9
  118.0 1.5 collective-permute-start.10
  119.5 4.9 %collective-permute-start.11 = (f32[5,1,18,130]{3,2,1,0:T(8,128)S(1)}, f32[5,1,18,130]{3,2,1,0:T(8,128)S(1)}, u32[]{:S(2)}, u32[]{:S(2)}) collective-permute-start(f32[5,1,18,130]{3,2,1,0:T(8,128)S(1)} %get-tuple-element.69), channel_id=1, source_target_pairs={{0,1},{1,2},{2,3},{4,5},{5,6},{6,7},{8,9},{9,10},{10,11},{12,13},{... | collective-permute-start | bytes 140408 | tf_op jit(solution)/shard_map/ppermute | solution.py:29
  124.5 1.1 broadcast_multiply_fusion.1
  125.6 1.3 collective-permute-done.11
  126.9 3.1 %broadcast_multiply_fusion = (f32[5,32,16,128]{3,2,1,0:T(8,128)S(1)}, f32[5,32,16,128]{3,2,1,0:T(8,128)S(1)}) fusion(f32[5,1,18,130]{3,2,1,0:T(8,128)S(1)} %collective-permute-done.10, f32[5,32,1,130]{3,2,1,0:T(1,128)S(1)} %collective-permute-done.8, f32[5,32,16,1]{3,2,1,0:T(8,128)S(1)} %copy-done.4, f32[5,32,16,128]{3,2,1,0:T(8,128)S(1)} %multiply_add_fusion, ...), kind=kLoop, calls=%fused_computation.48 | loop fusion | flops 5242880 | bytes 4212640 | tf_op jit(solution)/shard_map/mul | solution.py:64
  130.3 5.0 %add_multiply_fusion = f32[5,32,16,128]{3,2,1,0:T(8,128)S(1)} fusion(f32[5,32,16,128]{3,2,1,0:T(8,128)S(1)} %broadcast_dynamic-update-slice_fusion, f32[5,32,16,128]{3,2,1,0:T(8,128)S(1)} %multiply_add_fusion, f32[5,32,16,128]{3,2,1,0:T(8,128)S(1)} %copy-done.1, f32[32,16,128]{2,1,0:T(8,128)S(1)} %get-tuple-element.82, ...), kind=kLoop, calls=%fused_computation.44 | loop fusion | flops 14090240 | bytes 6320564 | tf_op jit(solution)/shard_map/mul | solution.py:162
  135.3 1.0 copy-done.7
  136.4 11.8 %gather_fusion = f32[2048]{0:T(1024)S(1)} fusion(f32[65536]{0:T(1024)S(1)} %bitcast.152, s32[2048]{0:T(1024)S(1)} %broadcast_clamp_fusion), kind=kCustom, calls=%fused_computation | custom fusion | bytes 24576 | tf_op jit(solution)/shard_map/gather | solution.py:164
  148.2 25.7 %all-gather.1 = f32[32768]{0:T(1024)S(1)} all-gather(f32[2048]{0:T(1024)S(1)} %gather_fusion), channel_id=3, replica_groups=mesh['stream'=8,'span'=16,'vert'=4] {'span'}, dimensions={0}, use_global_device_ids=true | all-gather | bytes 139264 | tf_op jit(solution)/shard_map/all_gather | solution.py:166
  174.1 10.6 %while.11 = (s32[]{:T(128)}, f32[3,64]{1,0:T(4,128)S(1)}, f32[16,3,2048]{2,0,1:T(8,128)S(1)}, s32[16,2048]{1,0:T(8,128)S(1)}, s32[]{:T(128)}, /*index=5*/s32[]{:T(128)}) while((s32[]{:T(128)}, f32[3,64]{1,0:T(4,128)S(1)}, f32[16,3,2048]{2,0,1:T(8,128)S(1)}, s32[16,2048]{1,0:T(8,128)S(1)}, s32[]{:T(128)}, /*index=5*/s32[]{:T(128)}) %tuple.46), condition=%wide.region_5.6_spmd.clone, body=%wide.region_4.5_spmd.clone.sunk | while | flops 4850051 | bytes 99927 | solution.py:109
  184.8 73.9 %psum.7 = f32[32]{0:T(128)} all-reduce(f32[32]{0:T(128)S(1)} %convolution_bitcast_fusion.1), channel_id=1, replica_groups=mesh['stream'=8,'span'=16,'vert'=4] {'stream','vert'}, use_global_device_ids=true, to_apply=%region_6.7 | all-reduce | flops 32 | bytes 256 | tf_op jit(solution)/shard_map/psum | solution.py:170
  (129 shorter events, 15.0 us)
Async XLA Ops:
  0.6 184.1 %copy-start = (f32[3,64,32]{1,2,0:T(8,128)S(1)}, f32[3,64,32]{1,2,0:T(8,128)}, u32[]{:S(2)}) copy-start(f32[3,64,32]{1,2,0:T(8,128)} %param.20) | copy-start | bytes 73732
  2.8 7.1 %copy-start.14 = (s32[64,1]{0,1:T(1,128)S(1)}, s32[64,1]{0,1:T(1,128)}, u32[]{:S(2)}) copy-start(s32[64,1]{0,1:T(1,128)} %param.16) | copy-start | bytes 772
  2.8 7.4 %copy-start.11 = (f32[64,5,256]{2,0,1:T(8,128)S(1)}, f32[64,5,256]{2,0,1:T(8,128)}, u32[]{:S(2)}) copy-start(f32[64,5,256]{2,0,1:T(8,128)} %param.15) | copy-start | bytes 983044
  3.4 25.8 %collective-permute-start = (f32[5,32,16,1]{1,2,3,0:T(8,128)S(1)}, f32[5,32,16,1]{1,2,3,0:T(8,128)S(1)}, u32[]{:S(2)}, u32[]{:S(2)}) collective-permute-start(f32[5,32,16,1]{1,2,3,0:T(8,128)S(1)} %copy.55), channel_id=1, source_target_pairs={{64,0},{128,64},{192,128},{256,192},{320,256},{384,320},{448,384},... | collective-permute-start | bytes 30728 | tf_op jit(solution)/shard_map/ppermute | solution.py:32
  6.4 23.5 %collective-permute-start.1 = (f32[5,32,16,1]{1,2,3,0:T(8,128)S(1)}, f32[5,32,16,1]{1,2,3,0:T(8,128)S(1)}, u32[]{:S(2)}, u32[]{:S(2)}) collective-permute-start(f32[5,32,16,1]{1,2,3,0:T(8,128)S(1)} %copy.56), channel_id=1, source_target_pairs={{0,64},{64,128},{128,192},{192,256},{256,320},{320,384},{384,448},... | collective-permute-start | bytes 30728 | tf_op jit(solution)/shard_map/ppermute | solution.py:29
  10.7 15.7 %copy-start.1 = (f32[5,32,16,128]{3,2,1,0:T(8,128)S(1)}, f32[5,32,16,128]{3,2,1,0:T(8,128)}, u32[]{:S(2)}) copy-start(f32[5,32,16,128]{3,2,1,0:T(8,128)} %param.13) | copy-start | bytes 3932164
  12.2 15.1 %copy-start.13 = (s32[1,1,1,2048]{3,2,1,0:T(1,128)S(1)}, s32[1,1,1,2048]{3,2,1,0:T(1,128)}, u32[]{:S(2)}) copy-start(s32[1,1,1,2048]{3,2,1,0:T(1,128)} %param.17) | copy-start | bytes 24580
  12.2 42.6 %all-to-all-start = ((f32[64,1,2560]{2,1,0:T(1,128)}), f32[64,1,2560]{2,1,0:T(1,128)}, u32[]{:S(2)}, u32[]{:S(2)}) async-start(f32[64,1,2560]{2,1,0:T(1,128)} %all_to_all.8), calls=%async_computation | async-start | bytes 1310720 | tf_op jit(solution)/shard_map/all_to_all | solution.py:133
  29.9 17.9 %copy-start.2 = (f32[5,32,16,1]{3,2,1,0:T(8,128)}, f32[5,32,16,1]{3,2,1,0:T(8,128)S(1)}, u32[]{:S(2)}) copy-start(f32[5,32,16,1]{3,2,1,0:T(8,128)S(1)} %copy.37) | copy-start | bytes 30724
  31.6 7.8 %copy-start.3 = (f32[5,32,16,1]{3,2,1,0:T(8,128)S(1)}, f32[5,32,16,1]{3,2,1,0:T(8,128)}, u32[]{:S(2)}) copy-start(f32[5,32,16,1]{3,2,1,0:T(8,128)} %copy.39) | copy-start | bytes 30724
  34.0 4.4 %collective-permute-start.2 = (f32[5,32,1,130]{3,2,1,0:T(1,128)S(1)}, f32[5,32,1,130]{3,2,1,0:T(1,128)S(1)}, u32[]{:S(2)}, u32[]{:S(2)}) collective-permute-start(f32[5,32,1,130]{3,2,1,0:T(1,128)S(1)} %get-tuple-element.80), channel_id=1, source_target_pairs={{4,0},{8,4},{12,8},{16,12},{20,16},{24,20},{28,24},{32,28},{36,32}... | collective-permute-start | bytes 249608 | tf_op jit(solution)/shard_map/ppermute | solution.py:32
  35.3 4.0 %collective-permute-start.3 = (f32[5,32,1,130]{3,2,1,0:T(1,128)S(1)}, f32[5,32,1,130]{3,2,1,0:T(1,128)S(1)}, u32[]{:S(2)}, u32[]{:S(2)}) collective-permute-start(f32[5,32,1,130]{3,2,1,0:T(1,128)S(1)} %get-tuple-element.79), channel_id=1, source_target_pairs={{0,4},{4,8},{8,12},{12,16},{16,20},{20,24},{24,28},{28,32},{32,36}... | collective-permute-start | bytes 249608 | tf_op jit(solution)/shard_map/ppermute | solution.py:29
  39.5 7.2 %collective-permute-start.4 = (f32[5,1,18,130]{3,2,1,0:T(8,128)S(1)}, f32[5,1,18,130]{3,2,1,0:T(8,128)S(1)}, u32[]{:S(2)}, u32[]{:S(2)}) collective-permute-start(f32[5,1,18,130]{3,2,1,0:T(8,128)S(1)} %get-tuple-element.72), channel_id=1, source_target_pairs={{1,0},{2,1},{3,2},{5,4},{6,5},{7,6},{9,8},{10,9},{11,10},{13,12},{... | collective-permute-start | bytes 140408 | tf_op jit(solution)/shard_map/ppermute | solution.py:32
  40.9 7.0 %collective-permute-start.5 = (f32[5,1,18,130]{3,2,1,0:T(8,128)S(1)}, f32[5,1,18,130]{3,2,1,0:T(8,128)S(1)}, u32[]{:S(2)}, u32[]{:S(2)}) collective-permute-start(f32[5,1,18,130]{3,2,1,0:T(8,128)S(1)} %get-tuple-element.71), channel_id=1, source_target_pairs={{0,1},{1,2},{2,3},{4,5},{5,6},{6,7},{8,9},{9,10},{10,11},{12,13},{... | collective-permute-start | bytes 140408 | tf_op jit(solution)/shard_map/ppermute | solution.py:29
  46.7 4.3 %copy-start.6 = (f32[32,16,128]{2,1,0:T(8,128)S(1)}, f32[32,16,128]{2,1,0:T(8,128)}, u32[]{:S(2)}) copy-start(f32[32,16,128]{2,1,0:T(8,128)} %param.14) | copy-start | bytes 786436
  46.7 4.3 %copy-start.8 = (f32[5,1,18,130]{3,2,1,0:T(8,128)}, f32[5,1,18,130]{3,2,1,0:T(8,128)S(1)}, u32[]{:S(2)}) copy-start(f32[5,1,18,130]{3,2,1,0:T(8,128)S(1)} %collective-permute-done.4) | copy-start | bytes 140404
  47.8 3.2 %copy-start.9 = (f32[5,1,18,130]{3,2,1,0:T(8,128)}, f32[5,1,18,130]{3,2,1,0:T(8,128)S(1)}, u32[]{:S(2)}) copy-start(f32[5,1,18,130]{3,2,1,0:T(8,128)S(1)} %collective-permute-done.5) | copy-start | bytes 140404
  57.4 26.4 %copy-start.16 = (f32[5]{0:T(128)S(1)}, f32[5]{0:T(128)}, u32[]{:S(2)}) copy-start(f32[5]{0:T(128)} %constant.116.clone) | copy-start | bytes 64
  57.5 26.5 %copy-start.15 = (f32[5]{0:T(128)S(1)}, f32[5]{0:T(128)}, u32[]{:S(2)}) copy-start(f32[5]{0:T(128)} %constant.117.clone) | copy-start | bytes 64
  93.4 9.7 %copy-start.12 = (s32[1,16,1,2048]{3,2,1,0:T(1,128)S(1)}, s32[1,16,1,2048]{3,2,1,0:T(1,128)}, u32[]{:S(2)}) copy-start(s32[1,16,1,2048]{3,2,1,0:T(1,128)} %param.19) | copy-start | bytes 393220
  95.3 7.8 %collective-permute-start.6 = (f32[5,32,16,1]{1,2,3,0:T(8,128)S(1)}, f32[5,32,16,1]{1,2,3,0:T(8,128)S(1)}, u32[]{:S(2)}, u32[]{:S(2)}) collective-permute-start(f32[5,32,16,1]{1,2,3,0:T(8,128)S(1)} %copy.44), channel_id=1, source_target_pairs={{64,0},{128,64},{192,128},{256,192},{320,256},{384,320},{448,384},... | collective-permute-start | bytes 30728 | tf_op jit(solution)/shard_map/ppermute | solution.py:32
  100.8 7.1 %collective-permute-start.7 = (f32[5,32,16,1]{1,2,3,0:T(8,128)S(1)}, f32[5,32,16,1]{1,2,3,0:T(8,128)S(1)}, u32[]{:S(2)}, u32[]{:S(2)}) collective-permute-start(f32[5,32,16,1]{1,2,3,0:T(8,128)S(1)} %copy.46), channel_id=1, source_target_pairs={{0,64},{64,128},{128,192},{192,256},{256,320},{320,384},{384,448},... | collective-permute-start | bytes 30728 | tf_op jit(solution)/shard_map/ppermute | solution.py:29
  109.5 8.4 %copy-start.5 = (f32[5,32,16,1]{3,2,1,0:T(8,128)S(1)}, f32[5,32,16,1]{3,2,1,0:T(8,128)}, u32[]{:S(2)}) copy-start(f32[5,32,16,1]{3,2,1,0:T(8,128)} %copy.47) | copy-start | bytes 30724
  112.3 5.5 %copy-start.4 = (f32[5,32,16,1]{3,2,1,0:T(8,128)S(1)}, f32[5,32,16,1]{3,2,1,0:T(8,128)}, u32[]{:S(2)}) copy-start(f32[5,32,16,1]{3,2,1,0:T(8,128)} %copy.45) | copy-start | bytes 30724
  112.4 4.5 %collective-permute-start.8 = (f32[5,32,1,130]{3,2,1,0:T(1,128)S(1)}, f32[5,32,1,130]{3,2,1,0:T(1,128)S(1)}, u32[]{:S(2)}, u32[]{:S(2)}) collective-permute-start(f32[5,32,1,130]{3,2,1,0:T(1,128)S(1)} %get-tuple-element.76), channel_id=1, source_target_pairs={{4,0},{8,4},{12,8},{16,12},{20,16},{24,20},{28,24},{32,28},{36,32}... | collective-permute-start | bytes 249608 | tf_op jit(solution)/shard_map/ppermute | solution.py:32
  113.8 4.0 %collective-permute-start.9 = (f32[5,32,1,130]{3,2,1,0:T(1,128)S(1)}, f32[5,32,1,130]{3,2,1,0:T(1,128)S(1)}, u32[]{:S(2)}, u32[]{:S(2)}) collective-permute-start(f32[5,32,1,130]{3,2,1,0:T(1,128)S(1)} %get-tuple-element.75), channel_id=1, source_target_pairs={{0,4},{4,8},{8,12},{12,16},{16,20},{20,24},{24,28},{28,32},{32,36}... | collective-permute-start | bytes 249608 | tf_op jit(solution)/shard_map/ppermute | solution.py:29
  118.0 7.5 %collective-permute-start.10 = (f32[5,1,18,130]{3,2,1,0:T(8,128)S(1)}, f32[5,1,18,130]{3,2,1,0:T(8,128)S(1)}, u32[]{:S(2)}, u32[]{:S(2)}) collective-permute-start(f32[5,1,18,130]{3,2,1,0:T(8,128)S(1)} %get-tuple-element.70), channel_id=1, source_target_pairs={{1,0},{2,1},{3,2},{5,4},{6,5},{7,6},{9,8},{10,9},{11,10},{13,12},{... | collective-permute-start | bytes 140408 | tf_op jit(solution)/shard_map/ppermute | solution.py:32
  119.5 7.4 %collective-permute-start.11 = (f32[5,1,18,130]{3,2,1,0:T(8,128)S(1)}, f32[5,1,18,130]{3,2,1,0:T(8,128)S(1)}, u32[]{:S(2)}, u32[]{:S(2)}) collective-permute-start(f32[5,1,18,130]{3,2,1,0:T(8,128)S(1)} %get-tuple-element.69), channel_id=1, source_target_pairs={{0,1},{1,2},{2,3},{4,5},{5,6},{6,7},{8,9},{9,10},{10,11},{12,13},{... | collective-permute-start | bytes 140408 | tf_op jit(solution)/shard_map/ppermute | solution.py:29
  135.3 1.1 copy-start.7
  136.4 37.5 %copy-start.10 = (f32[1,16,1,3,2048]{4,2,3,1,0:T(1,128)S(1)}, f32[1,16,1,3,2048]{4,2,3,1,0:T(1,128)}, u32[]{:S(2)}) copy-start(f32[1,16,1,3,2048]{4,2,3,1,0:T(1,128)} %param.18) | copy-start | bytes 1179652
